TPU v7x, 32 devices: a whole 2x2x4 slice. The times are simulated.
32 devices in a mesh: view: 4 (over y, x), tile: 8 (over z, core).
Axes of the slice: x: 2, y: 2, z: 4, core: 2. Of those that a mesh axis runs over, the one named last changes fastest.
Arguments:
- object_band: float32 [8, 2, 512, 128], P('view', None, 'tile'), may hold values from -6 to 6
- dual_band: float32 [8, 2, 512, 128], P('view', None, 'tile'), may hold values from -6 to 6
- probe_field: float32 [2, 128, 128], replicated, may hold values from -6 to 6
- positions: int32 [8, 256], P('view', 'tile'), may hold values from 0 to 63
- live_counts: int32 [8, 8], P('view', 'tile'), may hold values from 1 to 32, 85 in all within a row
- photon_counts: int32 [8, 256, 128, 128], P('view', 'tile'), may hold values from 0 to 1023
- footprints: int32 [8, 8], P('view', 'tile'), may hold values from 0 to 6
- weights: bfloat16 [8, 128, 65536], P('view', None, 'tile'), may hold values from -0.046875 to 0.046875
- volume: float32 [2, 512, 128, 128], P(None, 'tile'), may hold values from -6 to 6
Outputs:
- object_new: float32 [8, 2, 512, 128], P('view', None, 'tile')
- dual_new: float32 [8, 2, 512, 128], P('view', None, 'tile')
- volume_new: float32 [2, 512, 128, 128], P(None, 'tile')
Inputs may be any that keep to these rules, and one draw needn't show every extreme that they name: `positions`: offset of a slot's scan position from the first column of the tile that owns the slot. `live_counts`: the first that many of a tile's 32 slots are live; each view has exactly 85 live slots, and in each view some tile has all 32 live. `footprints`: first of the 2 consecutive detector tiles that a volume tile's shadow covers in a view.
All inputs are finite; a program needn't handle non-finite values. No bound on the sum of `live_counts` on one device may be relied on, other than what follows from the above.
Results may differ from a plain program's by a relative error of at most 0.006.
Values may be sent and summed in bfloat16 or wider, within the bound.
No kernel may reach another device: no remote copies, remote signals or barrier semaphores. Data moves between devices by JAX's collectives and lax.ppermute only.
A program may use at most 128 MiB of HBM per device.

v0:
```python
import jax
import jax.numpy as jnp
from jax import lax
from jax.sharding import PartitionSpec as P

rho_weight = 0.5
step_size = 0.5
prior_weight = 0.5
floor_term = 0.25


def passed_along(value, axis, steps):
    count = lax.axis_size(axis)
    initial, last = (max(0, -steps), min(count, count - steps))
    return lax.ppermute(value, axis, [(source, source + steps) for source in range(initial, last)])


def extended(array, sides, width):
    for axis, dim in sides:
        devices, length = (lax.axis_size(axis), array.shape[dim])
        up = [(i, (i + 1) % devices) for i in range(devices - 1)]
        down = [(j, i) for i, j in up]
        last = lax.slice_in_dim(array, length - width, length, axis=dim)
        initial = lax.slice_in_dim(array, 0, width, axis=dim)
        before = lax.ppermute(last, axis, up)
        after = lax.ppermute(initial, axis, down)
        array = jnp.concatenate([before, array, after], axis=dim)
    return array


def tables(order_n):
    counter = jnp.arange(order_n, dtype=jnp.int32)
    phase_index = counter[:, None] * counter[None, :] % order_n
    angles = phase_index.astype(jnp.float32) * (2.0 * jnp.pi / order_n)
    scaling = 1.0 / jnp.sqrt(jnp.float32(order_n))
    return (jnp.cos(angles) * scaling, -jnp.sin(angles) * scaling)


def block_minus(parts):
    upper_half = jnp.concatenate([parts[0], -parts[1]], axis=1)
    lower_half = jnp.concatenate([parts[1], parts[0]], axis=1)
    return jnp.concatenate([upper_half, lower_half], axis=0).astype(jnp.bfloat16)


def block_plus(parts):
    upper_half = jnp.concatenate([parts[0], parts[1]], axis=1)
    lower_half = jnp.concatenate([-parts[1], parts[0]], axis=1)
    return jnp.concatenate([upper_half, lower_half], axis=0).astype(jnp.bfloat16)


def markov(padded):
    centre = padded[:, 1:-1, 1:-1, 1:-1]
    summed = jnp.zeros_like(centre)
    neighbours = (
        padded[:, 2:, 1:-1, 1:-1],
        padded[:, :-2, 1:-1, 1:-1],
        padded[:, 1:-1, 2:, 1:-1],
        padded[:, 1:-1, :-2, 1:-1],
        padded[:, 1:-1, 1:-1, 2:],
        padded[:, 1:-1, 1:-1, :-2],
    )
    for neighbour in neighbours:
        difference = centre - neighbour
        summed = summed + difference / jnp.sqrt(1.0 + difference * difference)
    return summed


def batch_update(windows, probe_field, counts_grid, dft_blocks):
    left_a, right_b, right_a, left_b = dft_blocks
    probe_re = probe_field[0]
    probe_im = probe_field[1]
    obj_re = windows[:, 0]
    obj_im = windows[:, 1]
    exit_wave = jnp.stack(
        [probe_re * obj_re - probe_im * obj_im, probe_re * obj_im + probe_im * obj_re], axis=1
    ).astype(jnp.bfloat16)
    num_slots = exit_wave.shape[0]
    num_cols = exit_wave.shape[2]
    num_rows = exit_wave.shape[3]
    columns_done = jnp.einsum(
        "ab,sbh->sah",
        left_a,
        exit_wave.reshape(num_slots, 2 * num_cols, num_rows),
        preferred_element_type=jnp.float32,
    ).astype(jnp.bfloat16)
    columns_done = (
        columns_done.reshape(num_slots, 2, num_cols, num_rows)
        .transpose(0, 2, 1, 3)
        .reshape(num_slots, num_cols, 2 * num_rows)
    )
    spectrum = jnp.einsum("sph,hq->spq", columns_done, right_b, preferred_element_type=jnp.float32)
    amplitude = jnp.sqrt(counts_grid.astype(jnp.float32)) / 16.0
    spec_re = spectrum[:, :, :num_rows]
    spec_im = spectrum[:, :, num_rows:]
    factor = amplitude / jnp.sqrt(spec_re * spec_re + spec_im * spec_im + floor_term)
    replaced = (spectrum * jnp.concatenate([factor, factor], axis=2)).astype(jnp.bfloat16)
    inverse_rows = jnp.einsum(
        "spq,qh->sph", replaced, right_a, preferred_element_type=jnp.float32
    ).astype(jnp.bfloat16)
    inverse_rows = (
        inverse_rows.reshape(num_slots, num_cols, 2, num_rows)
        .transpose(0, 2, 1, 3)
        .reshape(num_slots, 2 * num_cols, num_rows)
    )
    new_wave = jnp.einsum(
        "ab,sbh->sah", left_b, inverse_rows, preferred_element_type=jnp.float32
    ).reshape(num_slots, 2, num_cols, num_rows)
    difference = new_wave - exit_wave.astype(jnp.float32)
    diff_re = difference[:, 0]
    diff_im = difference[:, 1]
    power = jnp.broadcast_to(probe_re * probe_re + probe_im * probe_im, diff_re.shape)
    return jnp.stack(
        [probe_re * diff_re + probe_im * diff_im, probe_re * diff_im - probe_im * diff_re, power],
        axis=2,
    )


def place_windows(shadows, footprints, tile_cols, band_cols):
    placed = []
    for view_index in range(shadows.shape[0]):
        blank = jnp.zeros((shadows.shape[1], band_cols, shadows.shape[3]), jnp.float32)
        first_col = footprints[view_index, 0] * tile_cols
        placed.append(lax.dynamic_update_slice_in_dim(blank, shadows[view_index], first_col, 1))
    return jnp.stack(placed)


def cut_windows(full_band, footprints, tile_cols, foot_cols):
    pieces = []
    for view_index in range(full_band.shape[0]):
        first_col = footprints[view_index, 0] * tile_cols
        pieces.append(lax.dynamic_slice_in_dim(full_band[view_index], first_col, foot_cols, 1))
    return jnp.stack(pieces)


def per_device(
    object_band,
    dual_band,
    probe_field,
    positions,
    live_counts,
    photon_counts,
    footprints,
    weights,
    volume,
):
    views_here = object_band.shape[0]
    tile_cols = object_band.shape[2]
    band_rows = object_band.shape[3]
    patch_cols = probe_field.shape[1]
    slots_here = positions.shape[1]
    band_cols = tile_cols * lax.axis_size("tile")
    foot_cols = weights.shape[1]
    voxels_here = weights.shape[2]
    depth_rows = volume.shape[2]
    dft_blocks = (
        block_minus(tables(patch_cols)),
        block_plus(tables(band_rows)),
        block_minus(tables(band_rows)),
        block_plus(tables(patch_cols)),
    )
    volume_low = volume.astype(jnp.bfloat16).reshape(2, voxels_here, band_rows)
    shadows = jnp.einsum("acx,kxh->akch", weights, volume_low, preferred_element_type=jnp.float32)
    placed = place_windows(shadows, footprints, tile_cols, band_cols)
    projection = lax.psum_scatter(placed, "tile", scatter_dimension=2, tiled=True)
    ahead_one = passed_along(object_band, "tile", -1)
    ahead_two = passed_along(object_band, "tile", -2)
    reach = jnp.concatenate([object_band, ahead_one, ahead_two], axis=2)
    slot_rank = jnp.arange(slots_here, dtype=jnp.int32)
    patch_rank = jnp.arange(patch_cols, dtype=jnp.int32)
    reach_rank = jnp.arange(3 * tile_cols, dtype=jnp.int32)
    updates = []
    for view_index in range(views_here):
        view_reach = reach[view_index]
        offsets = positions[view_index]
        windows = jax.vmap(
            lambda offset_col: lax.dynamic_slice_in_dim(view_reach, offset_col, patch_cols, 1)
        )(offsets)
        contrib = batch_update(windows, probe_field, photon_counts[view_index], dft_blocks)
        is_live = (slot_rank < live_counts[view_index, 0]).astype(jnp.float32)
        target_col = offsets[:, None] + patch_rank[None, :]
        placement = (target_col[:, :, None] == reach_rank[None, None, :]).astype(
            jnp.float32
        ) * is_live[:, None, None]
        placement = placement.reshape(slots_here * patch_cols, 3 * tile_cols)
        flat = contrib.reshape(slots_here * patch_cols, 3 * band_rows)
        gathered_cols = jnp.dot(
            placement.T, flat, precision=lax.Precision.HIGHEST, preferred_element_type=jnp.float32
        )
        updates.append(gathered_cols.reshape(3 * tile_cols, 3, band_rows).transpose(1, 0, 2))
    local_updates = jnp.stack(updates)
    own_part = local_updates[:, :, :tile_cols]
    from_one = passed_along(
        local_updates[:, :, tile_cols : 2 * tile_cols].astype(jnp.bfloat16), "tile", 1
    ).astype(jnp.float32)
    from_two = passed_along(
        local_updates[:, :, 2 * tile_cols :].astype(jnp.bfloat16), "tile", 2
    ).astype(jnp.float32)
    summed_update = own_part + from_one + from_two
    object_new = (
        object_band
        + summed_update[:, 0:2] / (1.0 + summed_update[:, 2:3])
        - rho_weight * (object_band - projection - dual_band)
    )
    dual_new = dual_band + projection - object_new
    residual = (projection - object_new + dual_band).astype(jnp.bfloat16)
    residual_full = lax.all_gather(residual, "tile", axis=2, tiled=True)
    residual_windows = cut_windows(residual_full, footprints, tile_cols, foot_cols)
    grad_part = jnp.einsum(
        "acx,akch->kxh", weights, residual_windows, preferred_element_type=jnp.float32
    ).reshape(2, tile_cols, depth_rows, band_rows)
    gradient = lax.psum(grad_part, "view")
    half_step = volume - step_size * gradient
    padded = extended(half_step, (("tile", 1),), 1)
    padded = jnp.pad(padded, ((0, 0), (0, 0), (1, 1), (1, 1)))
    volume_new = half_step - step_size * prior_weight * markov(padded)
    return (object_new, dual_new, volume_new)


def solution(mesh):
    return jax.shard_map(
        per_device,
        mesh=mesh,
        in_specs=(
            P("view", None, "tile", None),
            P("view", None, "tile", None),
            P(),
            P("view", "tile"),
            P("view", "tile"),
            P("view", "tile", None, None),
            P("view", "tile"),
            P("view", None, "tile"),
            P(None, "tile", None, None),
        ),
        out_specs=(
            P("view", None, "tile", None),
            P("view", None, "tile", None),
            P(None, "tile", None, None),
        ),
        check_vma=False,
    )
```

profile of v0, /device:TPU:1, one launch (start us, length us, event | category | flops | bytes accessed | tf_op | source)
XLA Modules:
  0.0 534.9 jit_solution(6786026787238977698)
XLA Ops:
  14.1 6.4 %convert_element_type.129 = bf16[2,64,128,128]{3,2,1,0:T(8,128)(2,1)} convert(f32[2,64,128,128]{3,2,1,0:T(8,128)} %param.17) | non-fusion elementwise | flops 2097152 | bytes 12582912 | tf_op jit(solution)/shard_map/convert_element_type | solution.py:161
  20.5 4.7 fusion.47
  29.9 6.9 %gather_fusion.1 = f32[32,2,128,128]{3,1,2,0:T(2,128)} fusion(f32[2,192,128]{2,0,1:T(2,128)S(1)} %get-tuple-element.23, s32[32]{0:T(128)S(1)} %get-tuple-element.36), kind=kCustom, calls=%fused_computation.1 | custom fusion | bytes 8388992 | tf_op jit(solution)/shard_map/vmap()/gather | solution.py:176
  36.8 9.9 %fusion.94 = (f32[32,1,128,128]{3,1,2,0:T(1,128)}, f32[32,1,128,128]{3,1,2,0:T(1,128)}) fusion(f32[32,2,128,128]{3,1,2,0:T(2,128)} %gather_fusion.1), kind=kLoop, calls=%fused_computation.162 | loop fusion | bytes 8388608 | tf_op jit(solution)/shard_map/slice | solution.py:73
  46.7 7.0 %gather_fusion = f32[32,2,128,128]{3,1,2,0:T(2,128)} fusion(f32[2,192,128]{2,0,1:T(2,128)S(1)} %get-tuple-element.24, s32[32]{0:T(128)S(1)} %get-tuple-element.37), kind=kCustom, calls=%fused_computation | custom fusion | bytes 8388992 | tf_op jit(solution)/shard_map/vmap()/gather | solution.py:176
  53.8 7.9 %fusion.95 = (f32[32,1,128,128]{3,1,2,0:T(1,128)S(1)}, f32[32,1,128,128]{3,1,2,0:T(1,128)S(1)}) fusion(f32[32,2,128,128]{3,1,2,0:T(2,128)} %gather_fusion), kind=kLoop, calls=%fused_computation.163 | loop fusion | bytes 8388608 | tf_op jit(solution)/shard_map/slice | solution.py:73
  71.8 8.0 %copy.103 = bf16[32,128,2,128]{3,2,1,0:T(2,128)(2,1)} copy(bf16[32,128,2,128]{1,2,3,0:T(2,128)(2,1)} %bitcast.198) | data formatting | bytes 4194304 | tf_op jit(solution)/shard_map/transpose | solution.py:88
  79.9 4.4 reshape.293
  84.2 4.4 fusion.83
  94.9 8.0 %copy.94 = bf16[32,128,2,128]{3,2,1,0:T(2,128)(2,1)} copy(bf16[32,128,2,128]{1,2,3,0:T(2,128)(2,1)} %bitcast.199) | data formatting | bytes 4194304 | tf_op jit(solution)/shard_map/transpose | solution.py:88
  122.3 8.0 %copy.104 = bf16[32,2,128,128]{2,1,3,0:T(2,128)(2,1)} copy(bf16[32,2,128,128]{3,1,2,0:T(2,128)(2,1)} %bitcast.200) | data formatting | bytes 4194304 | tf_op jit(solution)/shard_map/transpose | solution.py:102
  130.3 4.4 reshape.295
  138.7 8.0 %copy.95 = bf16[32,2,128,128]{2,1,3,0:T(2,128)(2,1)} copy(bf16[32,2,128,128]{3,1,2,0:T(2,128)(2,1)} %bitcast.201) | data formatting | bytes 4194304 | tf_op jit(solution)/shard_map/transpose | solution.py:102
  146.7 4.4 reshape.289
  155.4 5.7 %copy.96 = f32[32,256,128]{2,1,0:T(8,128)} copy(f32[32,256,128]{1,2,0:T(8,128)} %convolution_bitcast_fusion.2) | data formatting | bytes 8388608 | tf_op jit(solution)/shard_map/ab,sbh->sah/transpose | solution.py:105
  161.1 5.5 %convert_subtract_fusion = f32[32,2,128,128]{3,2,1,0:T(8,128)} fusion(f32[32,2,128,128]{3,2,1,0:T(8,128)} %bitcast.195, bf16[32,1,128,128]{3,2,1,0:T(8,128)(2,1)} %fusion.28, bf16[32,1,128,128]{3,2,1,0:T(8,128)(2,1)S(1)} %get-tuple-element.29), kind=kLoop, calls=%fused_computation.36 | loop fusion | flops 3145728 | bytes 10485760 | tf_op jit(solution)/shard_map/sub | solution.py:108
  169.4 5.7 %copy.105 = f32[32,256,128]{2,1,0:T(8,128)} copy(f32[32,256,128]{1,2,0:T(8,128)} %convolution_bitcast_fusion.1) | data formatting | bytes 8388608 | tf_op jit(solution)/shard_map/ab,sbh->sah/transpose | solution.py:105
  180.7 5.4 %pad_maximum_fusion = (f32[32,128,3,128]{3,1,0,2:T(8,128)}, f32[32,128,3,128]{3,1,0,2:T(8,128)}) fusion(f32[32,128,1,128]{3,1,0,2:T(8,128)S(1)} %stack_broadcast_in_dim.4, f32[32,128,1,128]{3,1,0,2:T(8,128)S(1)} %get-tuple-element.8, f32[32,128,1,128]{3,1,0,2:T(8,128)S(1)} %get-tuple-element.7, f32[32,128,1,128]{3,1,0,2:T(8,128)S(1)} %get-tuple-element.27, ...), kind=kLoop, calls=%fused_computation.12 | loop fusion | flops 6291456 | bytes 23068672 | tf_op jit(solution)/shard_map/stack | solution.py:112
  186.1 6.7 %copy.107 = f32[32,128,3,128]{1,0,3,2:T(8,128)} copy(f32[32,128,3,128]{3,1,0,2:T(8,128)} %get-tuple-element.19) | data formatting | bytes 12582912 | tf_op jit(solution)/shard_map/stack | solution.py:112
  192.8 11.4 %copy.132 = f32[48,8,32,128]{3,1,2,0:T(8,128)} copy(f32[48,8,32,128]{3,2,1,0:T(8,128)} %bitcast.189) | data formatting | bytes 12582912
  204.2 6.9 %copy.98 = f32[32,128,3,128]{1,0,3,2:T(8,128)} copy(f32[32,128,3,128]{3,1,0,2:T(8,128)} %get-tuple-element.20) | data formatting | bytes 12582912 | tf_op jit(solution)/shard_map/stack | solution.py:112
  211.1 8.9 %copy.133 = f32[48,8,32,128]{3,1,2,0:T(8,128)S(1)} copy(f32[48,8,32,128]{3,2,1,0:T(8,128)} %bitcast.190) | data formatting | bytes 12582912
  220.0 6.6 %fusion.44 = f32[1,3,192,128]{3,2,1,0:T(8,128)S(1)} fusion(f32[3,128,4096]{2,1,0:T(8,128)S(1)} %bitcast.187, f32[4096]{0:T(1024)S(1)} %broadcast_bitcast_fusion, s32[4096]{0:T(1024)S(1)} %get-tuple-element.44), kind=kOutput, calls=%fused_computation.85 | convolution fusion | flops 3625451520 | bytes 6619136 | tf_op jit(solution)/shard_map/dot_general | solution.py:186
  226.7 6.5 %fusion.41 = f32[1,3,192,128]{3,2,1,0:T(8,128)S(1)} fusion(f32[3,128,4096]{2,1,0:T(8,128)S(1)} %bitcast.188, f32[4096]{0:T(1024)S(1)} %broadcast_bitcast_fusion.1, s32[4096]{0:T(1024)S(1)} %get-tuple-element.45), kind=kOutput, calls=%fused_computation.84 | convolution fusion | flops 3625451520 | bytes 6619136 | tf_op jit(solution)/shard_map/dot_general | solution.py:186
  233.2 5.2 collective-permute-start.2
  245.1 15.8 %all_gather.3 = bf16[2,2,512,128]{3,2,1,0:T(8,128)(2,1)S(1)} all-gather(bf16[2,2,64,128]{3,2,1,0:T(8,128)(2,1)S(1)} %get-tuple-element.3), channel_id=1, replica_groups=mesh['view'=4,'tile'=8] {'tile'}, dimensions={2}, use_global_device_ids=true | all-gather | bytes 589824 | tf_op jit(solution)/shard_map/all_gather | solution.py:206
  261.0 6.9 %convolution_bitcast_fusion = f32[2,8192,128]{1,2,0:T(8,128)} fusion(bf16[2,128,8192]{2,1,0:T(8,128)(2,1)} %param.16, bf16[1,2,128,128]{3,2,1,0:T(8,128)(2,1)S(1)} %constant_dynamic-slice_fusion, bf16[1,2,128,128]{3,2,1,0:T(8,128)(2,1)S(1)} %constant_dynamic-slice_fusion.1), kind=kOutput, calls=%fused_computation.11 | convolution fusion | flops 1073807360 | bytes 12713984 | tf_op jit(solution)/shard_map/acx,akch->kxh/dot_general | solution.py:208
  267.8 8.9 %copy.119 = f32[2,8192,128]{2,1,0:T(8,128)} copy(f32[2,8192,128]{1,2,0:T(8,128)} %convolution_bitcast_fusion) | data formatting | bytes 16777216 | tf_op jit(solution)/shard_map/reshape | solution.py:210
  276.7 172.4 %all-reduce.3.cloned.1.call-done = f32[2,64,128,128]{3,2,1,0:T(8,128)} async-done(((f32[2,64,128,128]{3,2,1,0:T(8,128)}), f32[2,64,128,128]{3,2,1,0:T(8,128)}) %all-reduce.3.cloned.1.call-update) | async-done | bytes 8388624 | tf_op jit(solution)/shard_map/psum | solution.py:211
  449.2 11.9 %multiply_subtract_fusion.1 = f32[2,64,128,128]{3,2,1,0:T(8,128)} fusion(f32[2,64,128,128]{3,2,1,0:T(8,128)} %param.17, f32[2,64,128,128]{3,2,1,0:T(8,128)} %all-reduce.3.cloned.1.call-done), kind=kLoop, calls=%fused_computation.23 | loop fusion | flops 4194304 | bytes 25165824 | tf_op jit(solution)/shard_map/sub | solution.py:212
  472.2 15.4 %select_maximum_fusion = f32[2,66,130,130]{3,2,1,0:T(8,128)} fusion(f32[2,1,128,128]{3,2,1,0:T(8,128)S(1)} %collective-permute-done.4, f32[2,64,128,128]{3,2,1,0:T(8,128)} %multiply_subtract_fusion.1, f32[2,1,128,128]{3,2,1,0:T(8,128)S(1)} %collective-permute-done.5), kind=kLoop, calls=%fused_computation.6 | loop fusion | flops 33462000 | bytes 17573952 | tf_op jit(solution)/shard_map/concatenate | solution.py:27
  487.6 40.2 %multiply_subtract_fusion = f32[2,64,128,128]{3,2,1,0:T(8,128)} fusion(f32[2,64,128,128]{3,2,1,0:T(8,128)} %multiply_subtract_fusion.1, f32[2,66,130,130]{3,2,1,0:T(8,128)} %select_maximum_fusion, f32[2,1,128,128]{3,2,1,0:T(8,128)S(1)} %collective-permute-done.5, f32[2,1,128,128]{3,2,1,0:T(8,128)S(1)} %collective-permute-done.4), kind=kLoop, calls=%fused_computation.22 | loop fusion | flops 69206016 | bytes 50593792 | tf_op jit(solution)/shard_map/sub | solution.py:215
  (100 shorter events, 80.4 us)
Async XLA Ops:
  7.2 236.9 %reduce-scatter.2.cloned.1.call-start = ((), (), s32[]{:S(2)}) async-start(), calls=%async_computation.1 | async-start | bytes 1179648 | tf_op jit(solution)/shard_map/reduce_scatter | solution.py:164
  8.3 21.6 %collective-permute-start = (f32[2,2,64,128]{3,1,2,0:T(2,128)S(1)}, f32[2,2,64,128]{3,1,2,0:T(2,128)S(1)}, u32[]{:S(2)}, u32[]{:S(2)}) collective-permute-start(f32[2,2,64,128]{3,1,2,0:T(2,128)S(1)} %get-tuple-element.32), channel_id=1, source_target_pairs={{1,0},{2,1},{3,2},{4,3},{5,4},{6,5},{7,6},{9,8},{10,9},{11,10},{12... | collective-permute-start | bytes 393224 | tf_op jit(solution)/shard_map/ppermute | solution.py:15
  10.2 19.7 %collective-permute-start.1 = (f32[2,2,64,128]{3,1,2,0:T(2,128)S(1)}, f32[2,2,64,128]{3,1,2,0:T(2,128)S(1)}, u32[]{:S(2)}, u32[]{:S(2)}) collective-permute-start(f32[2,2,64,128]{3,1,2,0:T(2,128)S(1)} %get-tuple-element.32), channel_id=1, source_target_pairs={{2,0},{3,1},{4,2},{5,3},{6,4},{7,5},{10,8},{11,9},{12,10},{13,11},... | collective-permute-start | bytes 393224 | tf_op jit(solution)/shard_map/ppermute | solution.py:15
  25.2 1.8 copy-start.11
  25.2 1.9 copy-start.6
  25.2 1.9 copy-start.12
  26.5 422.7 %all-reduce.3.cloned.1.call-start = ((), (), s32[]{:S(2)}) async-start(), calls=%async_computation.2 | async-start | bytes 16777216 | tf_op jit(solution)/shard_map/psum | solution.py:211
  61.6 2.0 copy-start.4
  61.7 2.6 copy-start.5
  84.2 4.4 copy-start.2
  107.3 2.8 copy-start
  161.1 5.5 %copy-start.3 = (bf16[32,256,128]{1,2,0:T(8,128)(2,1)S(1)}, bf16[32,256,128]{1,2,0:T(8,128)(2,1)}, u32[]{:S(2)}) copy-start(bf16[32,256,128]{1,2,0:T(8,128)(2,1)} %reshape.295) | copy-start | bytes 6291460
  175.1 3.4 copy-start.1
  204.2 15.8 %slice-start = ((s8[6291456]{0:T(1024)(128)(4,1)}), s8[2097152]{0:T(1024)(128)(4,1)S(1)}, s32[]{:S(2)}) async-start(s8[6291456]{0:T(1024)(128)(4,1)} %bitcast.185), calls=%async_computation.3 | async-start | bytes 4194304
  211.1 8.9 %slice-start.1 = ((s8[6291456]{0:T(1024)(128)(4,1)}), s8[4194304]{0:T(1024)(128)(4,1)S(1)}, s32[]{:S(2)}) async-start(s8[6291456]{0:T(1024)(128)(4,1)} %bitcast.185), calls=%async_computation.4 | async-start | bytes 8388608
  226.7 17.5 %copy-start.7 = (f32[2,2,64,128]{3,2,1,0:T(8,128)S(1)}, f32[2,2,64,128]{3,2,1,0:T(8,128)}, u32[]{:S(2)}) copy-start(f32[2,2,64,128]{3,2,1,0:T(8,128)} %param.9) | copy-start | bytes 393220
  226.7 17.5 %copy-start.8 = (f32[2,2,64,128]{3,2,1,0:T(8,128)S(1)}, f32[2,2,64,128]{3,2,1,0:T(8,128)}, u32[]{:S(2)}) copy-start(f32[2,2,64,128]{3,2,1,0:T(8,128)} %param.10) | copy-start | bytes 393220
  233.2 8.9 %collective-permute-start.2 = (bf16[2,3,64,128]{3,2,1,0:T(8,128)(2,1)S(1)}, bf16[2,3,64,128]{3,2,1,0:T(8,128)(2,1)S(1)}, u32[]{:S(2)}, u32[]{:S(2)}) collective-permute-start(bf16[2,3,64,128]{3,2,1,0:T(8,128)(2,1)S(1)} %get-tuple-element.25), channel_id=1, source_target_pairs={{0,1},{1,2},{2,3},{3,4},{4,5},{5,6},{6,7},{8,9},{9,10},{10,11},{11... | collective-permute-start | bytes 294920 | tf_op jit(solution)/shard_map/ppermute | solution.py:15
  238.5 5.6 %collective-permute-start.3 = (bf16[2,3,64,128]{3,2,1,0:T(8,128)(2,1)S(1)}, bf16[2,3,64,128]{3,2,1,0:T(8,128)(2,1)S(1)}, u32[]{:S(2)}, u32[]{:S(2)}) collective-permute-start(bf16[2,3,64,128]{3,2,1,0:T(8,128)(2,1)S(1)} %get-tuple-element.26), channel_id=1, source_target_pairs={{0,2},{1,3},{2,4},{3,5},{4,6},{5,7},{8,10},{9,11},{10,12},{11,13},... | collective-permute-start | bytes 294920 | tf_op jit(solution)/shard_map/ppermute | solution.py:15
  245.1 222.8 %copy-start.10 = (f32[2,2,64,128]{3,2,1,0:T(8,128)}, f32[2,2,64,128]{3,2,1,0:T(8,128)S(1)}, u32[]{:S(2)}) copy-start(f32[2,2,64,128]{3,2,1,0:T(8,128)S(1)} %get-tuple-element.4) | copy-start | bytes 393220
  276.7 191.2 %copy-start.9 = (f32[2,2,64,128]{3,2,1,0:T(8,128)S(1)}, f32[2,2,64,128]{3,2,1,0:T(8,128)}, u32[]{:S(2)}) copy-start(f32[2,2,64,128]{3,2,1,0:T(8,128)} %reduce-scatter.2.cloned.1.call-done) | copy-start | bytes 393220
  462.1 6.5 %collective-permute-start.5 = (f32[2,1,128,128]{3,2,1,0:T(8,128)S(1)}, f32[2,1,128,128]{3,2,1,0:T(8,128)S(1)}, u32[]{:S(2)}, u32[]{:S(2)}) collective-permute-start(f32[2,1,128,128]{3,2,1,0:T(8,128)S(1)} %get-tuple-element.5), channel_id=1, source_target_pairs={{0,1},{1,2},{2,3},{3,4},{4,5},{5,6},{6,7},{8,9},{9,10},{10,11},{11... | collective-permute-start | bytes 393224 | tf_op jit(solution)/shard_map/ppermute | solution.py:25
  465.9 6.3 %collective-permute-start.4 = (f32[2,1,128,128]{3,2,1,0:T(8,128)S(1)}, f32[2,1,128,128]{3,2,1,0:T(8,128)S(1)}, u32[]{:S(2)}, u32[]{:S(2)}) collective-permute-start(f32[2,1,128,128]{3,2,1,0:T(8,128)S(1)} %get-tuple-element.6), channel_id=1, source_target_pairs={{1,0},{2,1},{3,2},{4,3},{5,4},{6,5},{7,6},{9,8},{10,9},{11,10},{12... | collective-permute-start | bytes 393224 | tf_op jit(solution)/shard_map/ppermute | solution.py:26
Sparse Core Ops, SparseCore 0:
  26.6 32.4 reduce-scatter.1
  276.8 172.2 all-reduce.2
where the time goes:
time: 540 us; the launch traced here: 535 us
  waiting for transfers between devices  178 us (33%)
  local copies, waits for them, and re-layouts  158 us (29%)
  other arithmetic  101 us (19%)
  matrix products  46.9 us (9%)
  starting transfers between devices  18.4 us (3%)
  between operations  16.2 us (3%)
  blocking collectives  15.8 us (3%)
    psum x1, waiting for transfers between devices, per_device(): gradient = lax.psum(grad_part, 'view')  172 us
    sub x1, other arithmetic, per_device(): volume_new = half_step - step_size * prior_weight * markov(padded)  40.2 us
    unnamed x34, local copies, waits for them, and re-layouts  23.5 us
    slice x2, local copies, waits for them, and re-layouts, batch_update(): obj_im = windows[:, 1]  17.8 us
    transpose x2, local copies, waits for them, and re-layouts, batch_update(): columns_done = columns_done.reshape(num_slots, 2, num_cols, num_rows).tra...  16 us
    transpose x2, local copies, waits for them, and re-layouts, batch_update(): inverse_rows = inverse_rows.reshape(num_slots, num_cols, 2, num_rows).tra...  16 us
    all_gather x1, blocking collectives, per_device(): residual_full = lax.all_gather(residual, 'tile', axis=2, tiled=True)  15.8 us
    concatenate x1, other arithmetic, extended(): array = jnp.concatenate([before, array, after], axis=dim)  15.4 us
  transfers between devices with their start and end apart: 8, of which 3 were waited for; matrix products, arithmetic and copies ran while one was open for 41% of the time, Pallas kernels for 0%

commit v1 on v0

--- a/solution.py
+++ b/solution.py
@@ -208,7 +208,9 @@
     grad_part = jnp.einsum(
         "acx,akch->kxh", weights, residual_windows, preferred_element_type=jnp.float32
     ).reshape(2, tile_cols, depth_rows, band_rows)
-    gradient = lax.psum(grad_part, "view")
+    gradient = grad_part
+    for hop in (1, 2):
+        gradient = gradient + lax.ppermute(gradient, "view", [(dev, dev ^ hop) for dev in range(4)])
     half_step = volume - step_size * gradient
     padded = extended(half_step, (("tile", 1),), 1)
     padded = jnp.pad(padded, ((0, 0), (0, 0), (1, 1), (1, 1)))

time: 540 us -> 735 us (1.36)
  waiting for transfers between devices: 178 us -> 367 us
    ppermute x0 -> x2, waiting for transfers between devices: none -> 361 us  [per_device(): lax.ppermute(gradient, 'view', [(dev, dev ^ hop) for dev in range(4)])]
    psum x1 -> x0, waiting for transfers between devices: 172 us -> none  [per_device(): gradient = lax.psum(grad_part, 'view')]
    add x0 -> x1, other arithmetic: none -> 11.9 us  [per_device(): gradient + lax.ppermute(gradient, 'view', [(dev, dev ^ hop) for dev in ra...]
    unnamed x34 -> x36, local copies, waits for them, and re-layouts: 23.5 us -> 23.5 us
  transfers between devices with their start and end apart: 8 -> 9, of which waited for: 3 -> 4; matrix products, arithmetic and copies ran while one was open for 41% -> 30% of each run, Pallas kernels for 0% -> 0%
where the time goes in v1:
time: 735 us; the launch traced here: 730 us
  waiting for transfers between devices  367 us (50%)
  local copies, waits for them, and re-layouts  158 us (21%)
  other arithmetic  105 us (14%)
  matrix products  47.1 us (6%)
  starting transfers between devices  21.2 us (3%)
  between operations  16.1 us (2%)
  blocking collectives  15.8 us (2%)
    ppermute x2, waiting for transfers between devices, per_device(): lax.ppermute(gradient, 'view', [(dev, dev ^ hop) for dev in range(4)])  361 us
    sub x1, other arithmetic, per_device(): volume_new = half_step - step_size * prior_weight * markov(padded)  39.8 us
    unnamed x36, local copies, waits for them, and re-layouts  23.5 us
    slice x2, local copies, waits for them, and re-layouts, batch_update(): obj_im = windows[:, 1]  17.7 us
    transpose x2, local copies, waits for them, and re-layouts, batch_update(): columns_done = columns_done.reshape(num_slots, 2, num_cols, num_rows).tra...  16 us
    transpose x2, local copies, waits for them, and re-layouts, batch_update(): inverse_rows = inverse_rows.reshape(num_slots, num_cols, 2, num_rows).tra...  16 us
    all_gather x1, blocking collectives, per_device(): residual_full = lax.all_gather(residual, 'tile', axis=2, tiled=True)  15.8 us
  transfers between devices with their start and end apart: 9, of which 4 were waited for; matrix products, arithmetic and copies ran while one was open for 30% of the time, Pallas kernels for 0%

profile of v1, /device:TPU:1, one launch (start us, length us, event | category | flops | bytes accessed | tf_op | source)
XLA Modules:
  0.0 730.0 jit_solution(10661013251693365148)
XLA Ops:
  14.1 6.4 convert_element_type.129
  20.5 4.7 fusion.47
  29.3 7.2 gather_fusion.1
  36.5 9.9 %fusion.94 = (f32[32,1,128,128]{3,1,2,0:T(1,128)}, f32[32,1,128,128]{3,1,2,0:T(1,128)}) fusion(f32[32,2,128,128]{3,1,2,0:T(2,128)} %gather_fusion.1), kind=kLoop, calls=%fused_computation.162 | loop fusion | bytes 8388608 | tf_op jit(solution)/shard_map/slice | solution.py:73
  46.4 7.4 %gather_fusion = f32[32,2,128,128]{3,1,2,0:T(2,128)} fusion(f32[2,192,128]{2,0,1:T(2,128)S(1)} %get-tuple-element.24, s32[32]{0:T(128)S(1)} %get-tuple-element.37), kind=kCustom, calls=%fused_computation | custom fusion | bytes 8388992 | tf_op jit(solution)/shard_map/vmap()/gather | solution.py:176
  53.8 7.9 %fusion.95 = (f32[32,1,128,128]{3,1,2,0:T(1,128)S(1)}, f32[32,1,128,128]{3,1,2,0:T(1,128)S(1)}) fusion(f32[32,2,128,128]{3,1,2,0:T(2,128)} %gather_fusion), kind=kLoop, calls=%fused_computation.163 | loop fusion | bytes 8388608 | tf_op jit(solution)/shard_map/slice | solution.py:73
  71.9 8.0 %copy.106 = bf16[32,128,2,128]{3,2,1,0:T(2,128)(2,1)} copy(bf16[32,128,2,128]{1,2,3,0:T(2,128)(2,1)} %bitcast.199) | data formatting | bytes 4194304 | tf_op jit(solution)/shard_map/transpose | solution.py:88
  94.9 8.0 %copy.97 = bf16[32,128,2,128]{3,2,1,0:T(2,128)(2,1)} copy(bf16[32,128,2,128]{1,2,3,0:T(2,128)(2,1)} %bitcast.200) | data formatting | bytes 4194304 | tf_op jit(solution)/shard_map/transpose | solution.py:88
  122.0 8.0 %copy.107 = bf16[32,2,128,128]{2,1,3,0:T(2,128)(2,1)} copy(bf16[32,2,128,128]{3,1,2,0:T(2,128)(2,1)} %bitcast.201) | data formatting | bytes 4194304 | tf_op jit(solution)/shard_map/transpose | solution.py:102
  130.0 4.4 reshape.295
  138.4 8.0 %copy.98 = bf16[32,2,128,128]{2,1,3,0:T(2,128)(2,1)} copy(bf16[32,2,128,128]{3,1,2,0:T(2,128)(2,1)} %bitcast.202) | data formatting | bytes 4194304 | tf_op jit(solution)/shard_map/transpose | solution.py:102
  155.1 5.7 copy.99
  160.8 5.5 convert_subtract_fusion
  169.1 5.7 copy.108
  180.3 5.4 pad_maximum_fusion
  185.7 6.7 copy.110
  192.4 11.4 %copy.136 = f32[48,8,32,128]{3,1,2,0:T(8,128)} copy(f32[48,8,32,128]{3,2,1,0:T(8,128)} %bitcast.190) | data formatting | bytes 12582912
  203.8 6.9 copy.101
  210.7 8.9 %copy.137 = f32[48,8,32,128]{3,1,2,0:T(8,128)S(1)} copy(f32[48,8,32,128]{3,2,1,0:T(8,128)} %bitcast.191) | data formatting | bytes 12582912
  219.7 6.8 fusion.44
  226.6 6.5 fusion.41
  233.1 5.2 collective-permute-start.2
  245.0 15.8 %all_gather.3 = bf16[2,2,512,128]{3,2,1,0:T(8,128)(2,1)S(1)} all-gather(bf16[2,2,64,128]{3,2,1,0:T(8,128)(2,1)S(1)} %get-tuple-element.3), channel_id=1, replica_groups=mesh['view'=4,'tile'=8] {'tile'}, dimensions={2}, use_global_device_ids=true | all-gather | bytes 589824 | tf_op jit(solution)/shard_map/all_gather | solution.py:206
  260.9 6.9 convolution_bitcast_fusion
  267.7 9.1 %copy.123 = f32[2,8192,128]{2,1,0:T(8,128)} copy(f32[2,8192,128]{1,2,0:T(8,128)} %convolution_bitcast_fusion) | data formatting | bytes 16777216 | tf_op jit(solution)/shard_map/reshape | solution.py:210
  278.0 181.0 %collective-permute-done.4 = f32[2,64,128,128]{3,2,1,0:T(8,128)} collective-permute-done((f32[2,64,128,128]{3,2,1,0:T(8,128)}, f32[2,64,128,128]{3,2,1,0:T(8,128)}, u32[]{:S(2)}, u32[]{:S(2)}) %collective-permute-start.4) | collective-permute-done | bytes 8388640 | tf_op jit(solution)/shard_map/ppermute | solution.py:213
  459.0 11.9 %add.237 = f32[2,64,128,128]{3,2,1,0:T(8,128)} add(f32[2,64,128,128]{3,2,1,0:T(8,128)} %bitcast.185, f32[2,64,128,128]{3,2,1,0:T(8,128)} %collective-permute-done.4) | non-fusion elementwise | flops 2097152 | bytes 25165824 | tf_op jit(solution)/shard_map/add | solution.py:213
  472.1 180.0 %collective-permute-done.5 = f32[2,64,128,128]{3,2,1,0:T(8,128)S(1)} collective-permute-done((f32[2,64,128,128]{3,2,1,0:T(8,128)}, f32[2,64,128,128]{3,2,1,0:T(8,128)S(1)}, u32[]{:S(2)}, u32[]{:S(2)}) %collective-permute-start.5) | collective-permute-done | bytes 8388640 | tf_op jit(solution)/shard_map/ppermute | solution.py:213
  652.1 7.3 %multiply_subtract_fusion.1 = f32[2,64,128,128]{3,2,1,0:T(8,128)S(1)} fusion(f32[2,64,128,128]{3,2,1,0:T(8,128)} %param.17, f32[2,64,128,128]{3,2,1,0:T(8,128)} %add.237, f32[2,64,128,128]{3,2,1,0:T(8,128)S(1)} %collective-permute-done.5), kind=kLoop, calls=%fused_computation.23 | loop fusion | flops 6291456 | bytes 33554432 | tf_op jit(solution)/shard_map/sub | solution.py:214
  659.4 4.7 collective-permute-start.7
  670.5 12.8 %select_maximum_fusion = f32[2,66,130,130]{3,2,1,0:T(8,128)} fusion(f32[2,1,128,128]{3,2,1,0:T(8,128)S(1)} %collective-permute-done.6, f32[2,64,128,128]{3,2,1,0:T(8,128)S(1)} %multiply_subtract_fusion.1, f32[2,1,128,128]{3,2,1,0:T(8,128)S(1)} %collective-permute-done.7), kind=kLoop, calls=%fused_computation.6 | loop fusion | flops 33462000 | bytes 17573952 | tf_op jit(solution)/shard_map/concatenate | solution.py:27
  683.3 39.8 %multiply_subtract_fusion = f32[2,64,128,128]{3,2,1,0:T(8,128)} fusion(f32[2,64,128,128]{3,2,1,0:T(8,128)} %copy-done, f32[2,66,130,130]{3,2,1,0:T(8,128)} %select_maximum_fusion, f32[2,1,128,128]{3,2,1,0:T(8,128)S(1)} %collective-permute-done.7, f32[2,1,128,128]{3,2,1,0:T(8,128)S(1)} %collective-permute-done.6), kind=kLoop, calls=%fused_computation.22 | loop fusion | flops 69206016 | bytes 50593792 | tf_op jit(solution)/shard_map/sub | solution.py:217
  (104 shorter events, 90.3 us)
Async XLA Ops:
  7.2 236.8 %reduce-scatter.2.cloned.1.call-start = ((), (), s32[]{:S(2)}) async-start(), calls=%async_computation.1 | async-start | bytes 1179648 | tf_op jit(solution)/shard_map/reduce_scatter | solution.py:164
  8.3 21.0 %collective-permute-start = (f32[2,2,64,128]{3,1,2,0:T(2,128)S(1)}, f32[2,2,64,128]{3,1,2,0:T(2,128)S(1)}, u32[]{:S(2)}, u32[]{:S(2)}) collective-permute-start(f32[2,2,64,128]{3,1,2,0:T(2,128)S(1)} %get-tuple-element.32), channel_id=1, source_target_pairs={{1,0},{2,1},{3,2},{4,3},{5,4},{6,5},{7,6},{9,8},{10,9},{11,10},{12... | collective-permute-start | bytes 393224 | tf_op jit(solution)/shard_map/ppermute | solution.py:15
  10.2 19.1 %collective-permute-start.1 = (f32[2,2,64,128]{3,1,2,0:T(2,128)S(1)}, f32[2,2,64,128]{3,1,2,0:T(2,128)S(1)}, u32[]{:S(2)}, u32[]{:S(2)}) collective-permute-start(f32[2,2,64,128]{3,1,2,0:T(2,128)S(1)} %get-tuple-element.32), channel_id=1, source_target_pairs={{2,0},{3,1},{4,2},{5,3},{6,4},{7,5},{10,8},{11,9},{12,10},{13,11},... | collective-permute-start | bytes 393224 | tf_op jit(solution)/shard_map/ppermute | solution.py:15
  25.2 1.2 copy-start.12
  25.2 1.3 copy-start.7
  25.2 1.3 copy-start.13
  61.7 2.0 copy-start.5
  61.7 2.6 copy-start.6
  84.2 4.4 copy-start.3
  107.3 2.8 copy-start.1
  160.8 5.5 copy-start.4
  174.7 3.4 copy-start.2
  203.8 15.8 %slice-start = ((s8[6291456]{0:T(1024)(128)(4,1)}), s8[2097152]{0:T(1024)(128)(4,1)S(1)}, s32[]{:S(2)}) async-start(s8[6291456]{0:T(1024)(128)(4,1)} %bitcast.186), calls=%async_computation.2 | async-start | bytes 4194304
  210.7 8.9 %slice-start.1 = ((s8[6291456]{0:T(1024)(128)(4,1)}), s8[4194304]{0:T(1024)(128)(4,1)S(1)}, s32[]{:S(2)}) async-start(s8[6291456]{0:T(1024)(128)(4,1)} %bitcast.186), calls=%async_computation.3 | async-start | bytes 8388608
  226.5 17.5 %copy-start.8 = (f32[2,2,64,128]{3,2,1,0:T(8,128)S(1)}, f32[2,2,64,128]{3,2,1,0:T(8,128)}, u32[]{:S(2)}) copy-start(f32[2,2,64,128]{3,2,1,0:T(8,128)} %param.9) | copy-start | bytes 393220
  226.5 17.5 %copy-start.9 = (f32[2,2,64,128]{3,2,1,0:T(8,128)S(1)}, f32[2,2,64,128]{3,2,1,0:T(8,128)}, u32[]{:S(2)}) copy-start(f32[2,2,64,128]{3,2,1,0:T(8,128)} %param.10) | copy-start | bytes 393220
  233.1 8.9 %collective-permute-start.2 = (bf16[2,3,64,128]{3,2,1,0:T(8,128)(2,1)S(1)}, bf16[2,3,64,128]{3,2,1,0:T(8,128)(2,1)S(1)}, u32[]{:S(2)}, u32[]{:S(2)}) collective-permute-start(bf16[2,3,64,128]{3,2,1,0:T(8,128)(2,1)S(1)} %get-tuple-element.25), channel_id=1, source_target_pairs={{0,1},{1,2},{2,3},{3,4},{4,5},{5,6},{6,7},{8,9},{9,10},{10,11},{11... | collective-permute-start | bytes 294920 | tf_op jit(solution)/shard_map/ppermute | solution.py:15
  238.3 5.6 collective-permute-start.3
  245.0 421.1 %copy-start.11 = (f32[2,2,64,128]{3,2,1,0:T(8,128)}, f32[2,2,64,128]{3,2,1,0:T(8,128)S(1)}, u32[]{:S(2)}) copy-start(f32[2,2,64,128]{3,2,1,0:T(8,128)S(1)} %get-tuple-element.4) | copy-start | bytes 393220
  276.8 182.2 %collective-permute-start.4 = (f32[2,64,128,128]{3,2,1,0:T(8,128)}, f32[2,64,128,128]{3,2,1,0:T(8,128)}, u32[]{:S(2)}, u32[]{:S(2)}) collective-permute-start(f32[2,64,128,128]{3,2,1,0:T(8,128)} %bitcast.184), channel_id=1, source_target_pairs={{0,8},{8,0},{16,24},{24,16},{1,9},{9,1},{17,25},{25,17},{2,10},{10... | collective-permute-start | bytes 25165832 | tf_op jit(solution)/shard_map/ppermute | solution.py:213
  470.9 195.3 %copy-start.10 = (f32[2,2,64,128]{3,2,1,0:T(8,128)S(1)}, f32[2,2,64,128]{3,2,1,0:T(8,128)}, u32[]{:S(2)}) copy-start(f32[2,2,64,128]{3,2,1,0:T(8,128)} %reduce-scatter.2.cloned.1.call-done) | copy-start | bytes 393220
  470.9 181.2 %collective-permute-start.5 = (f32[2,64,128,128]{3,2,1,0:T(8,128)}, f32[2,64,128,128]{3,2,1,0:T(8,128)S(1)}, u32[]{:S(2)}, u32[]{:S(2)}) collective-permute-start(f32[2,64,128,128]{3,2,1,0:T(8,128)} %add.237), channel_id=1, source_target_pairs={{0,16},{8,24},{16,0},{24,8},{1,17},{9,25},{17,1},{25,9},{2,18},{10... | collective-permute-start | bytes 25165832 | tf_op jit(solution)/shard_map/ppermute | solution.py:213
  659.4 11.1 %copy-start = (f32[2,64,128,128]{3,2,1,0:T(8,128)}, f32[2,64,128,128]{3,2,1,0:T(8,128)S(1)}, u32[]{:S(2)}) copy-start(f32[2,64,128,128]{3,2,1,0:T(8,128)S(1)} %multiply_subtract_fusion.1) | copy-start | bytes 25165828
  659.4 7.4 %collective-permute-start.7 = (f32[2,1,128,128]{3,2,1,0:T(8,128)S(1)}, f32[2,1,128,128]{3,2,1,0:T(8,128)S(1)}, u32[]{:S(2)}, u32[]{:S(2)}) collective-permute-start(f32[2,1,128,128]{3,2,1,0:T(8,128)S(1)} %get-tuple-element.5), channel_id=1, source_target_pairs={{0,1},{1,2},{2,3},{3,4},{4,5},{5,6},{6,7},{8,9},{9,10},{10,11},{11... | collective-permute-start | bytes 393224 | tf_op jit(solution)/shard_map/ppermute | solution.py:25
  664.2 6.3 collective-permute-start.6
Sparse Core Ops, SparseCore 0:
  26.6 32.4 reduce-scatter.1
